TPU v7x, 128 devices: a whole 4x4x4 slice. The times are simulated.
128 devices in a mesh: ctx: 32 (over x, y, core), tp: 4 (over z).
Axes of the slice: x: 4, y: 4, z: 4, core: 2. Of those that a mesh axis runs over, the one named last changes fastest.
Arguments:
- attention: bfloat16 [16384, 2048], P('ctx', 'tp'), may hold values from -6 to 6
- residual: bfloat16 [16384, 2048], P(('ctx', 'tp')), may hold values from -6 to 6
- w_out: bfloat16 [2048, 2048], P('tp'), may hold values from -0.125 to 0.125
- w_qkv: bfloat16 [3072, 2048], P('tp'), may hold values from -0.125 to 0.125
- norm_moe: float32 [2048], replicated, may hold values from 0.25 to 1.75
- norm_attn: float32 [2048], replicated, may hold values from 0.25 to 1.75
- expert_ids: int32 [16384, 4], P(('ctx', 'tp')), may hold values from 0 to 63, all different within a row; in each aligned block of 128 rows (0 to 127, 128 to 255, ...) at most 12 rows name the same one
- expert_gates: float32 [16384, 4], P(('ctx', 'tp')), may hold values from 0.02 to 0.3
- w_gate: bfloat16 [128, 2048, 384], P(('ctx', 'tp')), may hold values from -0.125 to 0.125
- w_up: bfloat16 [128, 2048, 384], P(('ctx', 'tp')), may hold values from -0.125 to 0.125
- w_down: bfloat16 [128, 384, 2048], P(('ctx', 'tp')), may hold values from -0.21875 to 0.21875
- d_projected: bfloat16 [16384, 3072], P('ctx', 'tp'), may hold values from -6 to 6
- d_stream: bfloat16 [16384, 2048], P(('ctx', 'tp')), may hold values from -6 to 6
Outputs:
- projected: bfloat16 [16384, 3072], P('ctx', 'tp')
- stream: bfloat16 [16384, 2048], P(('ctx', 'tp'))
- grad_attention: bfloat16 [16384, 2048], P('ctx', 'tp')
- grad_residual: bfloat16 [16384, 2048], P(('ctx', 'tp'))
- grad_w_out: bfloat16 [2048, 2048], P('tp', 'ctx')
- grad_w_gate: bfloat16 [128, 2048, 384], P(('ctx', 'tp'))
- grad_w_up: bfloat16 [128, 2048, 384], P(('ctx', 'tp'))
- grad_w_down: bfloat16 [128, 384, 2048], P(('ctx', 'tp'))
Inputs may be any that keep to these rules, and one draw needn't show every extreme that they name: `expert_ids`: each row names 4 different experts. Among the rows of one device no expert is named more than 12 times, a bound that some block reaches there.
All inputs are finite; a program needn't handle non-finite values.
Results may differ from a plain program's by a relative error of at most 0.0075.
Values may be sent and summed in bfloat16 or wider, within the bound.
No kernel may reach another device: no remote copies, remote signals or barrier semaphores. Data moves between devices by JAX's collectives and lax.ppermute only.
A program may use at most 128 MiB of HBM per device.

v0:
```python
import jax
import jax.numpy as jnp
from jax import lax
from jax.sharding import PartitionSpec as P

EPSILON = 1e-06


def swapped(block, axis, bit):
    count = lax.axis_size(axis)
    route = []
    for low in range(count):
        high = low | 1 << bit
        if high != low and high < count:
            route += [(low, high), (high, low)]
    return lax.ppermute(block, axis, route)


def rms_inverse(hidden):
    return lax.rsqrt(jnp.mean(hidden * hidden, axis=-1, keepdims=True) + EPSILON)


def rms_grad(hidden, gain_vec, inv_rms, grad_out):
    normed = hidden * inv_rms
    grad_normed = grad_out * gain_vec
    return inv_rms * (grad_normed - normed * jnp.mean(grad_normed * normed, axis=-1, keepdims=True))


def expert_inner(slot_rows, gate_mat, up_mat):
    pre_gate = jnp.dot(slot_rows, gate_mat, preferred_element_type=jnp.float32)
    pre_up = jnp.dot(slot_rows, up_mat, preferred_element_type=jnp.float32)
    active = (jax.nn.silu(pre_gate) * pre_up).astype(jnp.bfloat16)
    return (pre_gate, pre_up, active)


def half_backward(slot_rows, slot_grads, pre_gate, pre_up, active, gate_mat, up_mat, down_mat):
    sigmoid_gate = jax.nn.sigmoid(pre_gate)
    silu_gate = pre_gate * sigmoid_gate
    grad_active = jnp.einsum("sd,fd->sf", slot_grads, down_mat, preferred_element_type=jnp.float32)
    grad_gate = (
        grad_active * pre_up * sigmoid_gate * (1.0 + pre_gate * (1.0 - sigmoid_gate))
    ).astype(jnp.bfloat16)
    grad_up = (grad_active * silu_gate).astype(jnp.bfloat16)
    input_part = jnp.einsum("sf,df->sd", grad_gate, gate_mat, preferred_element_type=jnp.float32)
    input_part = (
        input_part + jnp.einsum("sf,df->sd", grad_up, up_mat, preferred_element_type=jnp.float32)
    ).astype(jnp.bfloat16)
    gate_term = jnp.einsum("sd,sf->df", slot_rows, grad_gate, preferred_element_type=jnp.float32)
    up_term = jnp.einsum("sd,sf->df", slot_rows, grad_up, preferred_element_type=jnp.float32)
    down_term = jnp.einsum("sf,sd->fd", active, slot_grads, preferred_element_type=jnp.float32)
    return (input_part, gate_term, up_term, down_term)


def tensor_rows(source, weights):
    return lax.psum_scatter(
        jnp.dot(source, weights, preferred_element_type=jnp.float32),
        "tp",
        scatter_dimension=0,
        tiled=True,
    )


def group_rows(local_rows):
    return lax.all_gather(local_rows, "tp", axis=0, tiled=True)


def dispatch_rows(payload):
    return lax.all_to_all(payload, ("ctx", "tp"), split_axis=0, concat_axis=0, tiled=True)


def return_rows(payload):
    return lax.all_to_all(payload, ("ctx", "tp"), split_axis=0, concat_axis=0, tiled=True)


def pair_share(rows):
    return swapped(rows, "tp", 0)


def pair_add(keep_part, give_part):
    received = swapped(give_part, "tp", 0)
    return (keep_part.astype(jnp.float32) + received.astype(jnp.float32)).astype(jnp.bfloat16)


def local(
    attention,
    residual,
    w_out,
    w_qkv,
    norm_moe,
    norm_attn,
    expert_ids,
    expert_gates,
    w_gate,
    w_up,
    w_down,
    d_projected,
    d_stream,
):
    ctx_count = lax.axis_size("ctx")
    tensor_count = lax.axis_size("tp")
    local_tokens = attention.shape[0] // tensor_count
    model_width = residual.shape[1]
    device_count = ctx_count * tensor_count
    expert_count = device_count // 2
    top_count = expert_ids.shape[1]
    capacity = 2 * max(1, local_tokens * top_count * 3 // (4 * expert_count))
    half_cap = capacity // 2
    slot_count = device_count * half_cap
    hidden = residual.astype(jnp.float32) + tensor_rows(attention, w_out)
    inv_one = rms_inverse(hidden)
    moe_input = (hidden * inv_one * norm_moe).astype(jnp.bfloat16)
    flat_ids = expert_ids.reshape(-1)
    expert_range = jnp.arange(expert_count, dtype=jnp.int32)
    onehot = (flat_ids[:, None] == expert_range[None, :]).astype(jnp.int32)
    position = jnp.sum((jnp.cumsum(onehot, axis=0) - onehot) * onehot, axis=1)
    slot_index = flat_ids * capacity + position
    slot_range = jnp.arange(expert_count * capacity, dtype=jnp.int32)
    matches = slot_index.reshape(local_tokens, top_count)[None, :, :] == slot_range[:, None, None]
    select = jnp.any(matches, axis=2).astype(jnp.bfloat16)
    gate_map = jnp.sum(jnp.where(matches, expert_gates[None, :, :], 0.0), axis=2)
    send_rows = jnp.dot(select, moe_input, preferred_element_type=jnp.float32).astype(jnp.bfloat16)
    arrived = dispatch_rows(send_rows.reshape(device_count, half_cap, model_width)).reshape(
        slot_count, model_width
    )
    gate_mine = w_gate[0]
    up_mine = w_up[0]
    down_mine = w_down[0]
    rows_full = jnp.concatenate([arrived, pair_share(arrived)], axis=0)
    pre_gate, pre_up, active = expert_inner(rows_full, gate_mine, up_mine)
    partial_value = jnp.dot(active, down_mine, preferred_element_type=jnp.float32).astype(
        jnp.bfloat16
    )
    produced = pair_add(partial_value[:slot_count], partial_value[slot_count:])
    returned = return_rows(produced.reshape(device_count, half_cap, model_width)).reshape(
        expert_count * capacity, model_width
    )
    picked = returned[slot_index].reshape(local_tokens, top_count, model_width)
    moe_out = jnp.sum(picked.astype(jnp.float32) * expert_gates[:, :, None], axis=1)
    stream_sum = hidden + moe_out
    stream = stream_sum.astype(jnp.bfloat16)
    inv_two = rms_inverse(stream_sum)
    attn_input = (stream_sum * inv_two * norm_attn).astype(jnp.bfloat16)
    attn_rows = group_rows(attn_input)
    projected = jnp.einsum(
        "td,od->to", attn_rows, w_qkv, preferred_element_type=jnp.float32
    ).astype(jnp.bfloat16)
    grad_attn_in = tensor_rows(d_projected, w_qkv)
    grad_stream = d_stream.astype(jnp.float32) + rms_grad(
        stream_sum, norm_attn, inv_two, grad_attn_in
    )
    grad_slots = jnp.dot(
        gate_map, grad_stream, precision=lax.Precision.HIGHEST, preferred_element_type=jnp.float32
    )
    grad_slots = grad_slots.astype(jnp.bfloat16).reshape(device_count, half_cap, model_width)
    grad_arrived = dispatch_rows(grad_slots).reshape(slot_count, model_width)
    grads_full = jnp.concatenate([grad_arrived, pair_share(grad_arrived)], axis=0)
    part_full, gate_grad, up_grad, down_grad = half_backward(
        rows_full, grads_full, pre_gate, pre_up, active, gate_mine, up_mine, down_mine
    )
    grad_input = pair_add(part_full[:slot_count], part_full[slot_count:])
    back_rows = return_rows(grad_input.reshape(device_count, half_cap, model_width)).reshape(
        expert_count * capacity, model_width
    )
    grad_moe_in = jnp.sum(
        back_rows[slot_index].reshape(local_tokens, top_count, model_width).astype(jnp.float32),
        axis=1,
    )
    grad_hidden = grad_stream + rms_grad(hidden, norm_moe, inv_one, grad_moe_in)
    grad_residual = grad_hidden.astype(jnp.bfloat16)
    grad_rows_all = group_rows(grad_residual)
    grad_attention = jnp.einsum(
        "td,kd->tk", grad_rows_all, w_out, preferred_element_type=jnp.float32
    ).astype(jnp.bfloat16)
    out_partial = jnp.einsum(
        "tk,td->kd", attention, grad_rows_all, preferred_element_type=jnp.float32
    )
    out_weight_grad = lax.psum_scatter(out_partial, "ctx", scatter_dimension=1, tiled=True)
    return (
        projected,
        stream,
        grad_attention,
        grad_residual,
        out_weight_grad.astype(jnp.bfloat16),
        gate_grad.astype(jnp.bfloat16)[None],
        up_grad.astype(jnp.bfloat16)[None],
        down_grad.astype(jnp.bfloat16)[None],
    )


def solution(mesh):
    in_specs = (
        P("ctx", "tp"),
        P(("ctx", "tp"), None),
        P("tp", None),
        P("tp", None),
        P(),
        P(),
        P(("ctx", "tp"), None),
        P(("ctx", "tp"), None),
        P(("ctx", "tp"), None, None),
        P(("ctx", "tp"), None, None),
        P(("ctx", "tp"), None, None),
        P("ctx", "tp"),
        P(("ctx", "tp"), None),
    )
    out_specs = (
        P("ctx", "tp"),
        P(("ctx", "tp"), None),
        P("ctx", "tp"),
        P(("ctx", "tp"), None),
        P("tp", "ctx"),
        P(("ctx", "tp"), None, None),
        P(("ctx", "tp"), None, None),
        P(("ctx", "tp"), None, None),
    )
    return jax.shard_map(local, mesh=mesh, in_specs=in_specs, out_specs=out_specs, check_vma=False)
```

profile of v0, /device:TPU:0, one launch (start us, length us, event | category | flops | bytes accessed | tf_op | source)
XLA Modules:
  0.0 913.7 jit_solution(2600129608861352997)
XLA Ops:
  7.2 5.1 fusion.25
  15.4 46.7 %reduce-scatter.4.cloned.1.call-done = f32[128,2048]{1,0:T(8,128)} async-done(((f32[512,2048]{1,0:T(8,128)}), f32[128,2048]{1,0:T(8,128)}) %reduce-scatter.4.cloned.1.call-update) | async-done | bytes 1048592 | tf_op jit(solution)/shard_map/reduce_scatter | solution.py:55
  63.7 4.1 convolution_convert_fusion.2
  67.8 6.2 reshape.127
  74.0 60.9 %all_to_all.20 = bf16[128,6,2048]{2,1,0:T(8,128)(2,1)} all-to-all(bf16[128,6,2048]{2,1,0:T(8,128)(2,1)} %reshape.127), channel_id=1, replica_groups=mesh['ctx'=32,'tp'=4] {'ctx','tp'}, dimensions={0} | all-to-all | bytes 6291456 | tf_op jit(solution)/shard_map/all_to_all | solution.py:68
  134.9 6.3 reshape.128
  142.2 5.0 fusion.26
  147.2 2.3 constant_dynamic-update-slice_fusion.1
  149.5 96.0 %collective-permute-done = bf16[768,2048]{1,0:T(8,128)(2,1)} collective-permute-done((bf16[768,2048]{1,0:T(8,128)(2,1)}, bf16[768,2048]{1,0:T(8,128)(2,1)}, u32[]{:S(2)}, u32[]{:S(2)}) %collective-permute-start) | collective-permute-done | bytes 3145760 | tf_op jit(solution)/shard_map/ppermute | solution.py:16
  245.6 2.3 constant_dynamic-update-slice_fusion
  247.9 3.4 fusion.12
  251.4 5.1 multiply_convert_fusion.2
  256.5 3.6 convolution_convert_fusion
  261.3 68.5 %collective-permute-done.1 = bf16[768,2048]{1,0:T(8,128)(2,1)S(1)} collective-permute-done((bf16[768,2048]{1,0:T(8,128)(2,1)S(1)}, bf16[768,2048]{1,0:T(8,128)(2,1)S(1)}, u32[]{:S(2)}, u32[]{:S(2)}) %collective-permute-start.1) | collective-permute-done | bytes 3145760 | tf_op jit(solution)/shard_map/ppermute | solution.py:16
  329.8 3.2 add_convert_fusion.2
  333.0 6.2 reshape.129
  339.2 6.0 all-to-all-start.1
  347.3 50.0 %all-to-all-done.1 = bf16[128,6,2048]{2,1,0:T(8,128)(2,1)} async-done(((bf16[128,6,2048]{2,1,0:T(8,128)(2,1)}), bf16[128,6,2048]{2,1,0:T(8,128)(2,1)}, u32[]{:S(2)}, u32[]{:S(2)}) %all-to-all-start.1) | async-done | bytes 3145760 | tf_op jit(solution)/shard_map/all_to_all | solution.py:72
  397.3 6.3 reshape.130
  403.6 7.6 gather_fusion
  411.2 4.8 reshape.135
  416.0 5.5 multiply_reduce_fusion
  426.7 8.3 convolution_convert_fusion.1
  435.0 6.3 reshape.131
  441.2 58.1 %all_to_all.21 = bf16[128,6,2048]{2,1,0:T(8,128)(2,1)} all-to-all(bf16[128,6,2048]{2,1,0:T(8,128)(2,1)} %reshape.131), channel_id=1, replica_groups=mesh['ctx'=32,'tp'=4] {'ctx','tp'}, dimensions={0} | all-to-all | bytes 6291456 | tf_op jit(solution)/shard_map/all_to_all | solution.py:68
  499.4 6.3 reshape.132
  509.2 67.2 %collective-permute-done.2 = bf16[768,2048]{1,0:T(8,128)(2,1)S(1)} collective-permute-done((bf16[768,2048]{1,0:T(8,128)(2,1)}, bf16[768,2048]{1,0:T(8,128)(2,1)S(1)}, u32[]{:S(2)}, u32[]{:S(2)}) %collective-permute-start.2) | collective-permute-done | bytes 3145760 | tf_op jit(solution)/shard_map/ppermute | solution.py:16
  576.9 4.4 multiply_convert_fusion
  581.4 3.5 fusion.10
  584.9 5.5 add_convert_fusion
  590.4 2.4 slice.32
  593.8 68.5 %collective-permute-done.3 = bf16[768,2048]{1,0:T(8,128)(2,1)S(1)} collective-permute-done((bf16[768,2048]{1,0:T(8,128)(2,1)S(1)}, bf16[768,2048]{1,0:T(8,128)(2,1)S(1)}, u32[]{:S(2)}, u32[]{:S(2)}) %collective-permute-start.3) | collective-permute-done | bytes 3145760 | tf_op jit(solution)/shard_map/ppermute | solution.py:16
  662.3 3.1 add_convert_fusion.1
  665.3 6.2 reshape.133
  671.6 58.3 %all_to_all.22 = bf16[128,6,2048]{2,1,0:T(8,128)(2,1)} all-to-all(bf16[128,6,2048]{2,1,0:T(8,128)(2,1)} %reshape.133), channel_id=1, replica_groups=mesh['ctx'=32,'tp'=4] {'ctx','tp'}, dimensions={0} | all-to-all | bytes 6291456 | tf_op jit(solution)/shard_map/all_to_all | solution.py:72
  729.9 6.3 reshape.134
  736.2 7.5 gather_fusion.1
  743.7 4.8 reshape.136
  748.5 5.8 reduce_sum.84
  756.9 3.2 add_convert_fusion.3
  760.9 25.9 %all-gather.5.cloned.1.call-done = bf16[512,2048]{1,0:T(8,128)(2,1)} async-done(((bf16[128,2048]{1,0:T(8,128)(2,1)}), bf16[512,2048]{1,0:T(8,128)(2,1)}) %all-gather.5.cloned.1.call-update) | async-done | bytes 2097168 | tf_op jit(solution)/shard_map/all_gather | solution.py:64
  786.8 4.9 convolution_bitcast_fusion
  791.8 7.1 fusion.2
  798.9 7.7 fusion.1
  806.6 4.6 fusion
  813.2 6.6 all-gather.3.cloned.1.call-done
  819.8 4.3 convolution_convert_fusion.6
  824.1 81.3 %reduce-scatter.8.cloned.1.call-done = f32[512,64]{0,1:T(8,128)} async-done(((f32[512,2048]{0,1:T(8,128)}), f32[512,64]{0,1:T(8,128)}) %reduce-scatter.8.cloned.1.call-update) | async-done | bytes 131088 | tf_op jit(solution)/shard_map/reduce_scatter | solution.py:177
  (130 shorter events, 25.7 us)
Async XLA Ops:
  7.2 135.0 %copy-start = (bf16[768,2048]{1,0:T(8,128)(2,1)S(1)}, bf16[768,2048]{1,0:T(8,128)(2,1)}, u32[]{:S(2)}) copy-start(bf16[768,2048]{1,0:T(8,128)(2,1)} %param.16) | copy-start | bytes 9437188
  7.2 54.9 %reduce-scatter.4.cloned.1.call-start = ((), (), s32[]{:S(2)}) async-start(), calls=%async_computation.7 | async-start | bytes 5242880 | tf_op jit(solution)/shard_map/reduce_scatter | solution.py:55
  12.4 51.3 %copy-start.22 = (f32[2048]{0:T(1024)S(1)}, f32[2048]{0:T(1024)}, u32[]{:S(2)}) copy-start(f32[2048]{0:T(1024)} %param.17) | copy-start | bytes 24580
  12.4 411.8 %reduce-scatter.6.cloned.1.call-start = ((), (), s32[]{:S(2)}) async-start(), calls=%async_computation.9 | async-start | bytes 5242880 | tf_op jit(solution)/shard_map/reduce_scatter | solution.py:55
  63.7 4.1 copy-start.27
  141.2 104.3 %collective-permute-start = (bf16[768,2048]{1,0:T(8,128)(2,1)}, bf16[768,2048]{1,0:T(8,128)(2,1)}, u32[]{:S(2)}, u32[]{:S(2)}) collective-permute-start(bf16[768,2048]{1,0:T(8,128)(2,1)} %reshape.128), channel_id=1, source_target_pairs={{0,1},{1,0},{2,3},{3,2},{4,5},{5,4},{6,7},{7,6},{8,9},{9,8},{10,11... | collective-permute-start | bytes 9437192 | tf_op jit(solution)/shard_map/ppermute | solution.py:16
  149.5 98.3 %copy-start.12 = (bf16[1,2048,384]{2,1,0:T(8,128)(2,1)S(1)}, bf16[1,2048,384]{2,1,0:T(8,128)(2,1)}, u32[]{:S(2)}) copy-start(bf16[1,2048,384]{2,1,0:T(8,128)(2,1)} %param.21) | copy-start | bytes 4718596
  247.9 3.5 copy-start.14
  247.9 3.5 copy-start.16
  251.4 5.1 copy-start.36
  251.4 5.1 copy-start.33
  256.5 3.7 copy-start.35
  260.4 69.4 %collective-permute-start.1 = (bf16[768,2048]{1,0:T(8,128)(2,1)S(1)}, bf16[768,2048]{1,0:T(8,128)(2,1)S(1)}, u32[]{:S(2)}, u32[]{:S(2)}) collective-permute-start(bf16[768,2048]{1,0:T(8,128)(2,1)S(1)} %slice.30), channel_id=1, source_target_pairs={{0,1},{1,0},{2,3},{3,2},{4,5},{5,4},{6,7},{7,6},{8,9},{9,8},{10,11... | collective-permute-start | bytes 9437192 | tf_op jit(solution)/shard_map/ppermute | solution.py:16
  339.2 6.2 copy-start.26
  339.2 58.1 %all-to-all-start.1 = ((bf16[128,6,2048]{2,1,0:T(8,128)(2,1)}), bf16[128,6,2048]{2,1,0:T(8,128)(2,1)}, u32[]{:S(2)}, u32[]{:S(2)}) async-start(bf16[128,6,2048]{2,1,0:T(8,128)(2,1)} %reshape.129), calls=%async_computation.2 | async-start | bytes 8388608 | tf_op jit(solution)/shard_map/all_to_all | solution.py:72
  345.2 441.6 %all-gather.5.cloned.1.call-start = ((), (), s32[]{:S(2)}) async-start(), calls=%async_computation.10 | async-start | bytes 2621440 | tf_op jit(solution)/shard_map/all_gather | solution.py:64
  346.4 57.3 %copy-start.24 = (s32[1024]{0:T(1024)}, s32[1024]{0:T(1024)S(1)}, u32[]{:S(2)}) copy-start(s32[1024]{0:T(1024)S(1)} %pad_clamp_fusion) | copy-start | bytes 12292
  416.0 5.5 copy-start.1
  416.0 5.6 copy-start.7
  421.6 2.7 copy-start.23
  424.2 2.5 copy-start.4
  424.2 2.5 copy-start.9
  505.7 70.8 %collective-permute-start.2 = (bf16[768,2048]{1,0:T(8,128)(2,1)}, bf16[768,2048]{1,0:T(8,128)(2,1)S(1)}, u32[]{:S(2)}, u32[]{:S(2)}) collective-permute-start(bf16[768,2048]{1,0:T(8,128)(2,1)} %reshape.132), channel_id=1, source_target_pairs={{0,1},{1,0},{2,3},{3,2},{4,5},{5,4},{6,7},{7,6},{8,9},{9,8},{10,11... | collective-permute-start | bytes 9437192 | tf_op jit(solution)/shard_map/ppermute | solution.py:16
  509.2 67.6 %copy-start.34 = (bf16[1,384,2048]{2,1,0:T(8,128)(2,1)S(1)}, bf16[1,384,2048]{2,1,0:T(8,128)(2,1)}, u32[]{:S(2)}) copy-start(bf16[1,384,2048]{2,1,0:T(8,128)(2,1)} %param.23) | copy-start | bytes 4718596
  509.2 67.6 %copy-start.37 = (f32[1536,384]{1,0:T(8,128)S(1)}, f32[1536,384]{1,0:T(8,128)}, u32[]{:S(2)}) copy-start(f32[1536,384]{1,0:T(8,128)} %copy-done.36) | copy-start | bytes 7077892
  509.2 67.6 %copy-start.38 = (f32[1536,384]{1,0:T(8,128)S(1)}, f32[1536,384]{1,0:T(8,128)}, u32[]{:S(2)}) copy-start(f32[1536,384]{1,0:T(8,128)} %get-tuple-element.17) | copy-start | bytes 7077892
  576.8 4.5 copy-start.15
  576.9 4.5 copy-start.13
  581.3 3.6 copy-start.18
  581.3 3.5 copy-start.20
  581.4 3.5 copy-start.17
  590.4 71.8 %copy-start.6 = (bf16[1536,2048]{1,0:T(8,128)(2,1)S(1)}, bf16[1536,2048]{1,0:T(8,128)(2,1)}, u32[]{:S(2)}) copy-start(bf16[1536,2048]{1,0:T(8,128)(2,1)} %add_convert_fusion) | copy-start | bytes 18874372
  592.9 69.4 %collective-permute-start.3 = (bf16[768,2048]{1,0:T(8,128)(2,1)S(1)}, bf16[768,2048]{1,0:T(8,128)(2,1)S(1)}, u32[]{:S(2)}, u32[]{:S(2)}) collective-permute-start(bf16[768,2048]{1,0:T(8,128)(2,1)S(1)} %slice.32), channel_id=1, source_target_pairs={{0,1},{1,0},{2,3},{3,2},{4,5},{5,4},{6,7},{7,6},{8,9},{9,8},{10,11... | collective-permute-start | bytes 9437192 | tf_op jit(solution)/shard_map/ppermute | solution.py:16
  729.9 6.3 copy-start.25
  748.5 5.8 copy-start.28
  754.4 2.2 copy-start.2
  754.4 2.3 copy-start.5
  754.4 2.5 copy-start.8
  754.4 2.5 copy-start.29
  754.4 2.4 copy-start.32
  760.1 59.7 %all-gather.3.cloned.1.call-start = ((), (), s32[]{:S(2)}) async-start(), calls=%async_computation.8 | async-start | bytes 2621440 | tf_op jit(solution)/shard_map/all_gather | solution.py:64
  760.7 144.7 %reduce-scatter.8.cloned.1.call-start = ((), (), s32[]{:S(2)}) async-start(), calls=%async_computation.11 | async-start | bytes 4325376 | tf_op jit(solution)/shard_map/reduce_scatter | solution.py:177
  791.7 7.1 copy-start.21
  791.7 14.8 %slice-start = ((s8[6291456]{0:T(1024)(128)(4,1)}), s8[4194304]{0:T(1024)(128)(4,1)S(1)}, s32[]{:S(2)}) async-start(s8[6291456]{0:T(1024)(128)(4,1)} %bitcast.72), calls=%async_computation.12 | async-start | bytes 8388608
  798.8 7.7 slice-start.1
  798.8 7.7 copy-start.19
  806.6 4.6 copy-start.10
  806.6 4.6 copy-start.11
  (3 other events, 2.2 us)
Sparse Core Ops, SparseCore 0:
  12.5 49.5 reduce-scatter.3
  147.3 75.6 reduce-scatter.5
  760.2 26.5 all-gather.4
  788.9 30.8 all-gather.2
  823.3 82.0 reduce-scatter.7
where the time goes:
time: 920 us; the launch traced here: 914 us
  waiting for transfers between devices  511 us (56%)
  blocking collectives  177 us (19%)
  local copies, waits for them, and re-layouts  89 us (10%)
  matrix products  78.7 us (9%)
  other arithmetic  32.3 us (4%)
  between operations  14.5 us (2%)
  starting transfers between devices  10.6 us (1%)
    ppermute x4, waiting for transfers between devices, swapped(): return lax.ppermute(block, axis, route)  300 us
    all_to_all x2, blocking collectives, dispatch_rows(): lax.all_to_all(payload, ('ctx', 'tp'), split_axis=0, concat_axis=0, tiled...  119 us
    reduce_scatter x1, waiting for transfers between devices, local(): lax.psum_scatter(out_partial, 'ctx', scatter_dimension=1, tiled=True)  81.3 us
    all_to_all x1, blocking collectives, return_rows(): lax.all_to_all(payload, ('ctx', 'tp'), split_axis=0, concat_axis=0, tiled...  58.3 us
    all_to_all x1, waiting for transfers between devices, return_rows(): lax.all_to_all(payload, ('ctx', 'tp'), split_axis=0, concat_axis=0, tiled...  50 us
    reduce_scatter x2, waiting for transfers between devices, tensor_rows(): lax.psum_scatter(jnp.dot(source, weights, preferred_element_type=jnp.floa...  46.7 us
    all_gather x2, waiting for transfers between devices, group_rows(): return lax.all_gather(local_rows, 'tp', axis=0, tiled=True)  32.4 us
  transfers between devices with their start and end apart: 10, of which 9 were waited for; matrix products, arithmetic and copies ran while one was open for 10% of the time, Pallas kernels for 0%

commit v1 on v0

--- a/solution.py
+++ b/solution.py
@@ -4,6 +4,11 @@
 from jax.sharding import PartitionSpec as P
 
 EPSILON = 1e-06
+
+
+def swapped_in(x, name, dim):
+    outgoing = jnp.stack([x] * lax.axis_size(name))
+    return jnp.concatenate(lax.all_to_all(outgoing, name, 0, 0), axis=dim)
 
 
 def swapped(block, axis, bit):
@@ -61,7 +66,7 @@
 
 
 def group_rows(local_rows):
-    return lax.all_gather(local_rows, "tp", axis=0, tiled=True)
+    return swapped_in(local_rows, "tp", 0)
 
 
 def dispatch_rows(payload):

time: 920 us -> 887 us (0.964)
  waiting for transfers between devices: 511 us -> 439 us
  blocking collectives: 177 us -> 207 us
    reduce_scatter x1, waiting for transfers between devices: 81.3 us -> 34.1 us  [local(): lax.psum_scatter(out_partial, 'ctx', scatter_dimension=1, tiled=True)]
    all_gather x2 -> x0, waiting for transfers between devices: 32.4 us -> none  [group_rows(): return lax.all_gather(local_rows, 'tp', axis=0, tiled=True)]
    all_to_all x0 -> x1, blocking collectives: none -> 29.5 us  [swapped_in(): return jnp.concatenate(lax.all_to_all(outgoing, name, 0, 0), axis=dim)]
  transfers between devices with their start and end apart: 10 -> 9, of which waited for: 9 -> 8; matrix products, arithmetic and copies ran while one was open for 10% -> 11% of each run, Pallas kernels for 0% -> 0%
where the time goes in v1:
time: 887 us; the launch traced here: 880 us
  waiting for transfers between devices  439 us (49%)
  blocking collectives  207 us (23%)
  local copies, waits for them, and re-layouts  92.1 us (10%)
  matrix products  80.4 us (9%)
  other arithmetic  32.1 us (4%)
  starting transfers between devices  15 us (2%)
  between operations  14.7 us (2%)
    ppermute x4, waiting for transfers between devices, swapped(): return lax.ppermute(block, axis, route)  300 us
    all_to_all x2, blocking collectives, dispatch_rows(): lax.all_to_all(payload, ('ctx', 'tp'), split_axis=0, concat_axis=0, tiled...  119 us
    all_to_all x1, blocking collectives, return_rows(): lax.all_to_all(payload, ('ctx', 'tp'), split_axis=0, concat_axis=0, tiled...  58.4 us
    all_to_all x1, waiting for transfers between devices, return_rows(): lax.all_to_all(payload, ('ctx', 'tp'), split_axis=0, concat_axis=0, tiled...  49.8 us
    reduce_scatter x2, waiting for transfers between devices, tensor_rows(): lax.psum_scatter(jnp.dot(source, weights, preferred_element_type=jnp.floa...  46.7 us
    reduce_scatter x1, waiting for transfers between devices, local(): lax.psum_scatter(out_partial, 'ctx', scatter_dimension=1, tiled=True)  34.1 us
    all_to_all x1, blocking collectives, swapped_in(): return jnp.concatenate(lax.all_to_all(outgoing, name, 0, 0), axis=dim)  29.5 us
  transfers between devices with their start and end apart: 9, of which 8 were waited for; matrix products, arithmetic and copies ran while one was open for 11% of the time, Pallas kernels for 0%

profile of v1, /device:TPU:0, one launch (start us, length us, event | category | flops | bytes accessed | tf_op | source)
XLA Modules:
  0.0 880.4 jit_solution(4808245127993687649)
XLA Ops:
  7.2 5.1 fusion.25
  15.4 46.7 %reduce-scatter.4.cloned.1.call-done = f32[128,2048]{1,0:T(8,128)} async-done(((f32[512,2048]{1,0:T(8,128)}), f32[128,2048]{1,0:T(8,128)}) %reduce-scatter.4.cloned.1.call-update) | async-done | bytes 1048592 | tf_op jit(solution)/shard_map/reduce_scatter | solution.py:60
  63.7 4.1 convolution_convert_fusion.2
  67.8 6.2 reshape.137
  74.0 60.9 %all_to_all.30 = bf16[128,6,2048]{2,1,0:T(8,128)(2,1)} all-to-all(bf16[128,6,2048]{2,1,0:T(8,128)(2,1)} %reshape.137), channel_id=1, replica_groups=mesh['ctx'=32,'tp'=4] {'ctx','tp'}, dimensions={0} | all-to-all | bytes 6291456 | tf_op jit(solution)/shard_map/all_to_all | solution.py:73
  134.9 6.3 reshape.138
  142.2 5.0 fusion.26
  147.2 2.3 constant_dynamic-update-slice_fusion.1
  149.5 96.0 %collective-permute-done = bf16[768,2048]{1,0:T(8,128)(2,1)} collective-permute-done((bf16[768,2048]{1,0:T(8,128)(2,1)}, bf16[768,2048]{1,0:T(8,128)(2,1)}, u32[]{:S(2)}, u32[]{:S(2)}) %collective-permute-start) | collective-permute-done | bytes 3145760 | tf_op jit(solution)/shard_map/ppermute | solution.py:21
  247.9 3.4 fusion.12
  251.4 5.1 multiply_convert_fusion.2
  256.5 3.6 convolution_convert_fusion
  261.3 68.5 %collective-permute-done.1 = bf16[768,2048]{1,0:T(8,128)(2,1)S(1)} collective-permute-done((bf16[768,2048]{1,0:T(8,128)(2,1)S(1)}, bf16[768,2048]{1,0:T(8,128)(2,1)S(1)}, u32[]{:S(2)}, u32[]{:S(2)}) %collective-permute-start.1) | collective-permute-done | bytes 3145760 | tf_op jit(solution)/shard_map/ppermute | solution.py:21
  329.8 3.2 add_convert_fusion.2
  333.0 6.3 reshape.139
  339.3 6.0 all-to-all-start.1
  347.5 49.8 %all-to-all-done.1 = bf16[128,6,2048]{2,1,0:T(8,128)(2,1)} async-done(((bf16[128,6,2048]{2,1,0:T(8,128)(2,1)}), bf16[128,6,2048]{2,1,0:T(8,128)(2,1)}, u32[]{:S(2)}, u32[]{:S(2)}) %all-to-all-start.1) | async-done | bytes 3145760 | tf_op jit(solution)/shard_map/all_to_all | solution.py:77
  397.3 6.3 reshape.140
  403.7 7.6 gather_fusion
  411.2 4.7 reshape.147
  415.9 5.5 multiply_reduce_fusion
  426.7 8.3 convolution_convert_fusion.1
  434.9 6.2 reshape.142
  441.2 58.1 %all_to_all.31 = bf16[128,6,2048]{2,1,0:T(8,128)(2,1)} all-to-all(bf16[128,6,2048]{2,1,0:T(8,128)(2,1)} %reshape.142), channel_id=1, replica_groups=mesh['ctx'=32,'tp'=4] {'ctx','tp'}, dimensions={0} | all-to-all | bytes 6291456 | tf_op jit(solution)/shard_map/all_to_all | solution.py:73
  499.3 6.3 reshape.143
  508.9 67.2 %collective-permute-done.2 = bf16[768,2048]{1,0:T(8,128)(2,1)S(1)} collective-permute-done((bf16[768,2048]{1,0:T(8,128)(2,1)}, bf16[768,2048]{1,0:T(8,128)(2,1)S(1)}, u32[]{:S(2)}, u32[]{:S(2)}) %collective-permute-start.2) | collective-permute-done | bytes 3145760 | tf_op jit(solution)/shard_map/ppermute | solution.py:21
  576.6 4.4 multiply_convert_fusion
  581.0 3.5 fusion.10
  584.6 5.5 add_convert_fusion
  590.1 2.4 slice.32
  593.5 68.5 %collective-permute-done.3 = bf16[768,2048]{1,0:T(8,128)(2,1)S(1)} collective-permute-done((bf16[768,2048]{1,0:T(8,128)(2,1)S(1)}, bf16[768,2048]{1,0:T(8,128)(2,1)S(1)}, u32[]{:S(2)}, u32[]{:S(2)}) %collective-permute-start.3) | collective-permute-done | bytes 3145760 | tf_op jit(solution)/shard_map/ppermute | solution.py:21
  661.9 3.1 add_convert_fusion.1
  665.0 6.2 reshape.144
  671.2 58.4 %all_to_all.32 = bf16[128,6,2048]{2,1,0:T(8,128)(2,1)} all-to-all(bf16[128,6,2048]{2,1,0:T(8,128)(2,1)} %reshape.144), channel_id=1, replica_groups=mesh['ctx'=32,'tp'=4] {'ctx','tp'}, dimensions={0} | all-to-all | bytes 6291456 | tf_op jit(solution)/shard_map/all_to_all | solution.py:77
  729.6 6.3 reshape.145
  735.9 7.5 gather_fusion.1
  743.5 4.8 reshape.148
  748.3 5.8 reduce_sum.84
  756.5 3.0 add_convert_fusion.3
  759.8 29.5 %all_to_all.33 = bf16[4,128,2048]{2,1,0:T(8,128)(2,1)S(1)} all-to-all(bf16[4,128,2048]{2,1,0:T(8,128)(2,1)S(1)} %stack.5), channel_id=1, replica_groups=mesh['ctx'=32,'tp'=4] {'tp'}, dimensions={0} | all-to-all | bytes 4194304 | tf_op jit(solution)/shard_map/all_to_all | solution.py:11
  790.7 3.2 convolution_bitcast_fusion
  794.0 7.0 fusion.2
  802.6 4.7 all-to-all-start.2
  807.4 8.0 fusion.1
  815.4 7.7 fusion
  825.2 8.3 all-to-all-done.2
  833.5 4.3 convolution_convert_fusion.6
  837.8 34.1 %reduce-scatter.8.cloned.1.call-done = f32[512,64]{0,1:T(8,128)} async-done(((f32[512,2048]{0,1:T(8,128)}), f32[512,64]{0,1:T(8,128)}) %reduce-scatter.8.cloned.1.call-update) | async-done | bytes 131088 | tf_op jit(solution)/shard_map/reduce_scatter | solution.py:182
  (130 shorter events, 30.4 us)
Async XLA Ops:
  7.2 135.1 %copy-start = (bf16[768,2048]{1,0:T(8,128)(2,1)S(1)}, bf16[768,2048]{1,0:T(8,128)(2,1)}, u32[]{:S(2)}) copy-start(bf16[768,2048]{1,0:T(8,128)(2,1)} %param.16) | copy-start | bytes 9437188
  7.2 54.9 %reduce-scatter.4.cloned.1.call-start = ((), (), s32[]{:S(2)}) async-start(), calls=%async_computation.9 | async-start | bytes 5242880 | tf_op jit(solution)/shard_map/reduce_scatter | solution.py:60
  12.4 51.3 %copy-start.25 = (f32[2048]{0:T(1024)S(1)}, f32[2048]{0:T(1024)}, u32[]{:S(2)}) copy-start(f32[2048]{0:T(1024)} %param.17) | copy-start | bytes 24580
  12.4 411.8 %reduce-scatter.6.cloned.1.call-start = ((), (), s32[]{:S(2)}) async-start(), calls=%async_computation.10 | async-start | bytes 5242880 | tf_op jit(solution)/shard_map/reduce_scatter | solution.py:60
  63.7 4.1 copy-start.30
  141.2 104.4 %collective-permute-start = (bf16[768,2048]{1,0:T(8,128)(2,1)}, bf16[768,2048]{1,0:T(8,128)(2,1)}, u32[]{:S(2)}, u32[]{:S(2)}) collective-permute-start(bf16[768,2048]{1,0:T(8,128)(2,1)} %reshape.138), channel_id=1, source_target_pairs={{0,1},{1,0},{2,3},{3,2},{4,5},{5,4},{6,7},{7,6},{8,9},{9,8},{10,11... | collective-permute-start | bytes 9437192 | tf_op jit(solution)/shard_map/ppermute | solution.py:21
  149.5 98.4 %copy-start.16 = (bf16[1,2048,384]{2,1,0:T(8,128)(2,1)S(1)}, bf16[1,2048,384]{2,1,0:T(8,128)(2,1)}, u32[]{:S(2)}) copy-start(bf16[1,2048,384]{2,1,0:T(8,128)(2,1)} %param.21) | copy-start | bytes 4718596
  247.9 3.5 copy-start.18
  247.9 3.5 copy-start.20
  251.4 5.1 copy-start.39
  251.4 5.1 copy-start.36
  256.5 3.7 copy-start.38
  260.4 69.4 %collective-permute-start.1 = (bf16[768,2048]{1,0:T(8,128)(2,1)S(1)}, bf16[768,2048]{1,0:T(8,128)(2,1)S(1)}, u32[]{:S(2)}, u32[]{:S(2)}) collective-permute-start(bf16[768,2048]{1,0:T(8,128)(2,1)S(1)} %slice.30), channel_id=1, source_target_pairs={{0,1},{1,0},{2,3},{3,2},{4,5},{5,4},{6,7},{7,6},{8,9},{9,8},{10,11... | collective-permute-start | bytes 9437192 | tf_op jit(solution)/shard_map/ppermute | solution.py:21
  339.3 6.4 copy-start.29
  339.3 58.0 %all-to-all-start.1 = ((bf16[128,6,2048]{2,1,0:T(8,128)(2,1)}), bf16[128,6,2048]{2,1,0:T(8,128)(2,1)}, u32[]{:S(2)}, u32[]{:S(2)}) async-start(bf16[128,6,2048]{2,1,0:T(8,128)(2,1)} %reshape.139), calls=%async_computation.2 | async-start | bytes 8388608 | tf_op jit(solution)/shard_map/all_to_all | solution.py:77
  345.2 526.7 %reduce-scatter.8.cloned.1.call-start = ((), (), s32[]{:S(2)}) async-start(), calls=%async_computation.11 | async-start | bytes 4325376 | tf_op jit(solution)/shard_map/reduce_scatter | solution.py:182
  346.6 57.1 %copy-start.27 = (s32[1024]{0:T(1024)}, s32[1024]{0:T(1024)S(1)}, u32[]{:S(2)}) copy-start(s32[1024]{0:T(1024)S(1)} %pad_clamp_fusion) | copy-start | bytes 12292
  415.9 5.5 copy-start.1
  415.9 5.6 copy-start.7
  421.5 2.7 copy-start.26
  424.2 2.5 copy-start.4
  424.2 2.5 copy-start.11
  505.6 70.5 %collective-permute-start.2 = (bf16[768,2048]{1,0:T(8,128)(2,1)}, bf16[768,2048]{1,0:T(8,128)(2,1)S(1)}, u32[]{:S(2)}, u32[]{:S(2)}) collective-permute-start(bf16[768,2048]{1,0:T(8,128)(2,1)} %reshape.143), channel_id=1, source_target_pairs={{0,1},{1,0},{2,3},{3,2},{4,5},{5,4},{6,7},{7,6},{8,9},{9,8},{10,11... | collective-permute-start | bytes 9437192 | tf_op jit(solution)/shard_map/ppermute | solution.py:21
  508.9 67.6 %copy-start.37 = (bf16[1,384,2048]{2,1,0:T(8,128)(2,1)S(1)}, bf16[1,384,2048]{2,1,0:T(8,128)(2,1)}, u32[]{:S(2)}) copy-start(bf16[1,384,2048]{2,1,0:T(8,128)(2,1)} %param.23) | copy-start | bytes 4718596
  508.9 67.6 %copy-start.40 = (f32[1536,384]{1,0:T(8,128)S(1)}, f32[1536,384]{1,0:T(8,128)}, u32[]{:S(2)}) copy-start(f32[1536,384]{1,0:T(8,128)} %copy-done.39) | copy-start | bytes 7077892
  508.9 67.6 %copy-start.41 = (f32[1536,384]{1,0:T(8,128)S(1)}, f32[1536,384]{1,0:T(8,128)}, u32[]{:S(2)}) copy-start(f32[1536,384]{1,0:T(8,128)} %get-tuple-element.17) | copy-start | bytes 7077892
  576.5 4.5 copy-start.19
  576.6 4.5 copy-start.17
  581.0 3.5 copy-start.22
  581.0 3.5 copy-start.24
  581.0 3.5 copy-start.21
  590.1 71.9 %copy-start.6 = (bf16[1536,2048]{1,0:T(8,128)(2,1)S(1)}, bf16[1536,2048]{1,0:T(8,128)(2,1)}, u32[]{:S(2)}) copy-start(bf16[1536,2048]{1,0:T(8,128)(2,1)} %add_convert_fusion) | copy-start | bytes 18874372
  592.5 69.4 %collective-permute-start.3 = (bf16[768,2048]{1,0:T(8,128)(2,1)S(1)}, bf16[768,2048]{1,0:T(8,128)(2,1)S(1)}, u32[]{:S(2)}, u32[]{:S(2)}) collective-permute-start(bf16[768,2048]{1,0:T(8,128)(2,1)S(1)} %slice.32), channel_id=1, source_target_pairs={{0,1},{1,0},{2,3},{3,2},{4,5},{5,4},{6,7},{7,6},{8,9},{9,8},{10,11... | collective-permute-start | bytes 9437192 | tf_op jit(solution)/shard_map/ppermute | solution.py:21
  729.6 6.3 copy-start.28
  748.3 5.8 copy-start.31
  754.1 2.2 copy-start.2
  754.1 2.3 copy-start.5
  754.1 2.5 copy-start.8
  754.1 2.5 copy-start.32
  754.1 2.4 copy-start.35
  759.5 29.8 %copy-start.12 = (bf16[128,2048]{1,0:T(8,128)(2,1)}, bf16[128,2048]{1,0:T(8,128)(2,1)S(1)}, u32[]{:S(2)}) copy-start(bf16[128,2048]{1,0:T(8,128)(2,1)S(1)} %get-tuple-element.12) | copy-start | bytes 1572868
  759.8 30.9 %copy-start.15 = (bf16[512,512]{1,0:T(8,128)(2,1)S(1)}, bf16[512,512]{1,0:T(8,128)(2,1)}, u32[]{:S(2)}) copy-start(bf16[512,512]{1,0:T(8,128)(2,1)} %param.13) | copy-start | bytes 1572868
  789.4 1.3 copy-start.9
  793.9 7.0 copy-start.13
  802.6 30.9 %all-to-all-start.2 = ((bf16[4,128,2048]{2,1,0:T(8,128)(2,1)}), bf16[4,128,2048]{2,1,0:T(8,128)(2,1)}, u32[]{:S(2)}, u32[]{:S(2)}) async-start(bf16[4,128,2048]{2,1,0:T(8,128)(2,1)} %stack.4), calls=%async_computation.3 | async-start | bytes 4194304 | tf_op jit(solution)/shard_map/all_to_all | solution.py:11
  807.3 8.0 copy-start.23
  815.4 7.8 copy-start.10
  815.4 7.8 copy-start.14
  (3 other events, 2.2 us)
Sparse Core Ops, SparseCore 0:
  12.5 49.5 reduce-scatter.3
  147.4 75.6 reduce-scatter.5
  794.1 77.8 reduce-scatter.7
